TPU v7x, 512 devices: a whole 4x4x16 slice. The times are simulated.
512 devices in a mesh: grp: 16 (over z_lo, core), seq: 32 (over x, z_hi, y).
Axes of the slice: x: 4, y: 4, z: 16 (z_hi: 2, z_lo: 8; z = z_hi * 8 + z_lo), core: 2. Of those that a mesh axis runs over, the one named last changes fastest.
Arguments:
- queries: bfloat16 [65536, 3072], P(('grp', 'seq')), may hold values from -6 to 6, as said below
- key_states: bfloat16 [65536, 3072], P(('grp', 'seq')), may hold values from -6 to 6
- value_states: bfloat16 [65536, 3072], P(('grp', 'seq')), may hold values from -16 to 16
- key_keep: int32 [65536], P(('grp', 'seq')), may hold values 0 or 1
- summary_pos: int32 [16], replicated, may hold values from 0 to 31
Outputs:
- attended: bfloat16 [65536, 3072], P(('grp', 'seq'))
Inputs may be any that keep to these rules, and one draw needn't show every extreme that they name: queries and key_states entries lie within -6 to 6.
All inputs are finite; a program needn't handle non-finite values. No bound on the sum of `key_keep` on one device may be relied on, other than what follows from the above.
Results may differ from a plain program's by a relative error of at most 0.008.
Values may be sent and summed in bfloat16 or wider, within the bound.
No kernel may reach another device: no remote copies, remote signals or barrier semaphores. Data moves between devices by JAX's collectives and lax.ppermute only.
A program may use at most 64 MiB of HBM per device.

v0:
```python
import math
import jax
import jax.numpy as jnp
from jax import lax
from jax.sharding import PartitionSpec as P

HEADS = 24
HEAD_DIM = 128
FIXED_HEADS = 4
STRIDED_HEADS = 4
LOCAL_HEADS = 16
BLOCK = 128
LOOKBACK = 2
NEG = -1e30


def passed_along(block, axis, distance):
    devices = range(lax.axis_size(axis))
    route = [(i - distance, i) for i in devices if i - distance in devices]
    return lax.ppermute(block, axis, route)


def spread(value, axis, source):
    kept = jnp.where(lax.axis_index(axis) == source, value, 0).astype(value.dtype)
    return lax.psum(kept, axis)


def partial_softmax(query_heads, key_rows, value_rows, allowed):
    scores = jnp.einsum(
        "qhd,khd->hqk", query_heads, key_rows, preferred_element_type=jnp.float32
    ) / math.sqrt(HEAD_DIM)
    scores = jnp.where(allowed[None], scores, NEG)
    row_max = jnp.max(scores, axis=2)
    weights = jnp.where(allowed[None], jnp.exp(scores - row_max[:, :, None]), 0.0)
    row_sum = jnp.sum(weights, axis=2)
    weighted = jnp.einsum(
        "hqk,khd->hqd", weights.astype(jnp.bfloat16), value_rows, preferred_element_type=jnp.float32
    )
    return (row_max, row_sum, weighted)


def merge_state(left_part, right_part):
    row_max = jnp.maximum(left_part[0], right_part[0])
    left_scale = jnp.exp(left_part[0] - row_max)
    right_scale = jnp.exp(right_part[0] - row_max)
    row_sum = left_part[1] * left_scale + right_part[1] * right_scale
    weighted = left_part[2] * left_scale[:, :, None] + right_part[2] * right_scale[:, :, None]
    return (row_max, row_sum, weighted)


def blank_state(count):
    return (
        jnp.full((count, BLOCK), NEG, jnp.float32),
        jnp.zeros((count, BLOCK), jnp.float32),
        jnp.zeros((count, BLOCK, HEAD_DIM), jnp.float32),
    )


def head_range(state, head_lo, head_hi):
    return tuple((member[head_lo:head_hi] for member in state))


def on_device(queries, key_states, value_states, key_keep, summary_pos):
    stride = lax.axis_size("seq")
    groups = lax.axis_size("grp")
    column = lax.axis_index("seq")
    window = lax.axis_index("grp")
    block_id = window * stride + column
    lane_ids = jnp.arange(BLOCK, dtype=jnp.int32)
    group_ids = jnp.arange(groups, dtype=jnp.int32)
    query_heads = queries.reshape(BLOCK, HEADS, HEAD_DIM)
    keep_flag = key_keep.astype(jnp.bfloat16)
    own_block = (key_states, value_states, keep_flag)

    def all_heads(block_rows, allowed):
        return partial_softmax(
            query_heads,
            block_rows[0].reshape(BLOCK, HEADS, HEAD_DIM),
            block_rows[1].reshape(BLOCK, HEADS, HEAD_DIM),
            allowed,
        )

    diagonal = lane_ids[:, None] == lane_ids[None, :]
    causal = (lane_ids[None, :] <= lane_ids[:, None]) & ((key_keep[None, :] == 1) | diagonal)
    near_state = all_heads(own_block, causal)
    prior_one = passed_along((own_block[0], own_block[1], own_block[2]), ("grp", "seq"), 1)
    prior_two = passed_along((own_block[0], own_block[1], own_block[2]), ("grp", "seq"), 2)
    for earlier in (prior_one, prior_two):
        allowed = jnp.broadcast_to((earlier[2] > 0)[None, :], (BLOCK, BLOCK))
        near_state = merge_state(near_state, all_heads(earlier, allowed))
    fixed_lo = LOCAL_HEADS * HEAD_DIM
    fixed_hi = (LOCAL_HEADS + FIXED_HEADS) * HEAD_DIM
    root_dev = summary_pos[window]
    summary_own = (key_states[:, fixed_lo:fixed_hi], value_states[:, fixed_lo:fixed_hi], keep_flag)
    summary_here = (
        spread(summary_own[0], "seq", root_dev),
        spread(summary_own[1], "seq", root_dev),
        spread(summary_own[2], "seq", root_dev),
    )
    fixed_queries = query_heads[:, LOCAL_HEADS : LOCAL_HEADS + FIXED_HEADS]
    shard_rows = (
        lax.all_gather(summary_here[0], "grp", axis=0, tiled=True),
        lax.all_gather(summary_here[1], "grp", axis=0, tiled=True),
        lax.all_gather(summary_here[2], "grp", axis=0, tiled=True),
    )
    row_count = shard_rows[0].shape[0]
    row_window = jnp.arange(row_count, dtype=jnp.int32) // BLOCK
    hit_mask = row_window[:, None] == group_ids[None, :]
    row_summary = jnp.sum(jnp.where(hit_mask, summary_pos[None, :], 0), axis=1)
    usable = (row_window * stride + row_summary < block_id - LOOKBACK) & (shard_rows[2] > 0)
    allowed = jnp.broadcast_to(usable[None, :], (BLOCK, row_count))
    term = partial_softmax(
        fixed_queries,
        shard_rows[0].reshape(row_count, FIXED_HEADS, HEAD_DIM),
        shard_rows[1].reshape(row_count, FIXED_HEADS, HEAD_DIM),
        allowed,
    )
    fixed_state = merge_state(blank_state(FIXED_HEADS), term)
    column_own = (key_states[:, fixed_hi:], value_states[:, fixed_hi:], keep_flag)
    strided_queries = query_heads[:, LOCAL_HEADS + FIXED_HEADS :]
    shard_rows = (
        lax.all_gather(column_own[0], "grp", axis=0, tiled=True),
        lax.all_gather(column_own[1], "grp", axis=0, tiled=True),
        lax.all_gather(column_own[2], "grp", axis=0, tiled=True),
    )
    row_count = shard_rows[0].shape[0]
    row_window = jnp.arange(row_count, dtype=jnp.int32) // BLOCK
    usable = (row_window < window) & (shard_rows[2] > 0)
    allowed = jnp.broadcast_to(usable[None, :], (BLOCK, row_count))
    term = partial_softmax(
        strided_queries,
        shard_rows[0].reshape(row_count, STRIDED_HEADS, HEAD_DIM),
        shard_rows[1].reshape(row_count, STRIDED_HEADS, HEAD_DIM),
        allowed,
    )
    strided_state = merge_state(blank_state(STRIDED_HEADS), term)
    local_total = head_range(near_state, 0, LOCAL_HEADS)
    fixed_total = merge_state(
        head_range(near_state, LOCAL_HEADS, LOCAL_HEADS + FIXED_HEADS), fixed_state
    )
    strided_total = merge_state(
        head_range(near_state, LOCAL_HEADS + FIXED_HEADS, HEADS), strided_state
    )
    row_sum = jnp.concatenate([local_total[1], fixed_total[1], strided_total[1]], axis=0)
    weighted = jnp.concatenate([local_total[2], fixed_total[2], strided_total[2]], axis=0)
    result = weighted / row_sum[:, :, None]
    return jnp.transpose(result, (1, 0, 2)).reshape(BLOCK, HEADS * HEAD_DIM).astype(jnp.bfloat16)


def solution(mesh):
    return jax.shard_map(
        on_device,
        mesh=mesh,
        in_specs=(
            P(("grp", "seq"), None),
            P(("grp", "seq"), None),
            P(("grp", "seq"), None),
            P(("grp", "seq")),
            P(),
        ),
        out_specs=P(("grp", "seq"), None),
        check_vma=False,
    )
```

profile of v0, /device:TPU:1, one launch (start us, length us, event | category | flops | bytes accessed | tf_op | source)
XLA Modules:
  0.0 1218.3 jit_solution(5872520702400437514)
XLA Ops:
  7.4 2.3 copy.80
  12.6 1.8 slice_select_fusion.1
  17.4 559.2 %all-reduce.3.cloned.1.call-done = (bf16[128,512]{0,1:T(8,128)(2,1)}, bf16[128,512]{0,1:T(8,128)(2,1)}) async-done(((bf16[128,512]{0,1:T(8,128)(2,1)}, bf16[128,512]{0,1:T(8,128)(2,1)}), (bf16[128,512]{0,1:T(8,128)(2,1)}, bf16[128,512]{0,1:T(8,128)(2,1)})) %all-reduce.3.cloned.1.call-update) | async-done | bytes 262160 | tf_op jit(solution)/shard_map/psum | solution.py:25
  576.7 2.1 collective-permute-start.2
  578.8 1.9 collective-permute-start.1
  580.7 1.9 collective-permute-start.5
  582.6 1.9 collective-permute-start.4
  584.6 1.9 collective-permute-start
  586.9 282.3 %psum.21 = bf16[128]{0:T(256)(128)(2,1)S(1)} all-reduce(bf16[128]{0:T(256)(128)(2,1)S(1)} %broadcast_select_fusion), channel_id=1, replica_groups=mesh['grp'=16,'seq'=32] {'seq'}, use_global_device_ids=true, to_apply=%region_4.5 | all-reduce | flops 128 | bytes 512 | tf_op jit(solution)/shard_map/psum | solution.py:25
  869.2 219.4 %all-gather = bf16[16,1,128]{2,1,0:T(2,128)(2,1)S(1)} all-gather(bf16[1,1,128]{2,1,0:T(2,128)(2,1)S(1)} %bitcast.74), channel_id=1, replica_groups=mesh['grp'=16,'seq'=32] {'grp'}, dimensions={0}, use_global_device_ids=true | all-gather | bytes 4352 | tf_op jit(solution)/shard_map/all_gather | solution.py:104
  1088.7 25.1 %all-gather.1 = bf16[16,1,128]{2,1,0:T(2,128)(2,1)S(1)} all-gather(bf16[1,1,128]{2,1,0:T(2,128)(2,1)S(1)} %get-tuple-element.36), channel_id=1, replica_groups=mesh['grp'=16,'seq'=32] {'grp'}, dimensions={0}, use_global_device_ids=true | all-gather | bytes 4352 | tf_op jit(solution)/shard_map/all_gather | solution.py:124
  1115.1 2.1 collective-permute-start.3
  1117.3 16.0 %collective-permute-done.3 = bf16[128]{0:T(256)(128)(2,1)S(1)} collective-permute-done((bf16[128]{0:T(256)(128)(2,1)S(1)}, bf16[128]{0:T(256)(128)(2,1)S(1)}, u32[]{:S(2)}, u32[]{:S(2)}) %collective-permute-start.3) | collective-permute-done | bytes 288 | tf_op jit(solution)/shard_map/ppermute | solution.py:20
  1134.8 2.3 copy.88
  1137.1 1.6 fusion.96
  1139.0 1.6 fusion.94
  1144.0 3.9 copy.101
  1147.9 2.7 fusion.2
  1150.7 2.0 copy-done.3
  1153.8 2.9 bitcast_reduce_fusion
  1156.8 1.6 fusion.5
  1160.4 1.7 fusion.55
  1162.1 43.3 %all-gather.9.cloned.1.call-done = bf16[2048,512]{0,1:T(8,128)(2,1)} async-done(((bf16[128,512]{0,1:T(8,128)(2,1)}), bf16[2048,512]{0,1:T(8,128)(2,1)}) %all-gather.9.cloned.1.call-update) | async-done | bytes 2097168 | tf_op jit(solution)/shard_map/all_gather | solution.py:103
  1205.4 4.0 fusion.56
  (71 shorter events, 16.6 us)
Async XLA Ops:
  7.4 569.2 %all-reduce.3.cloned.1.call-start = ((), (), s32[]{:S(2)}) async-start(), calls=%async_computation.4 | async-start | bytes 524288 | tf_op jit(solution)/shard_map/psum | solution.py:25
  7.4 3.9 copy-start.9
  9.7 574.9 %copy-start.10 = (s32[128]{0:T(128)S(1)}, s32[128]{0:T(128)}, u32[]{:S(2)}) copy-start(s32[128]{0:T(128)} %param.8) | copy-start | bytes 1540
  9.7 576.9 %copy-start.7 = (bf16[128,3072]{1,0:T(8,128)(2,1)S(1)}, bf16[128,3072]{1,0:T(8,128)(2,1)}, u32[]{:S(2)}) copy-start(bf16[128,3072]{1,0:T(8,128)(2,1)} %param.5) | copy-start | bytes 2359300
  12.6 1101.4 %copy-start.8 = (bf16[128,3072]{1,0:T(8,128)(2,1)S(1)}, bf16[128,3072]{1,0:T(8,128)(2,1)}, u32[]{:S(2)}) copy-start(bf16[128,3072]{1,0:T(8,128)(2,1)} %param.6) | copy-start | bytes 2359300
  15.1 1128.9 %all-gather.13.cloned.1.call-start = ((), (), s32[]{:S(2)}) async-start(), calls=%async_computation.3 | async-start | bytes 2228224 | tf_op jit(solution)/shard_map/all_gather | solution.py:123
  16.7 1131.2 %all-gather.11.cloned.1.call-start = ((), (), s32[]{:S(2)}) async-start(), calls=%async_computation.2 | async-start | bytes 2228224 | tf_op jit(solution)/shard_map/all_gather | solution.py:122
  17.3 1136.5 %all-gather.7.cloned.1.call-start = ((), (), s32[]{:S(2)}) async-start(), calls=%async_computation | async-start | bytes 2228224 | tf_op jit(solution)/shard_map/all_gather | solution.py:102
  576.6 628.8 %all-gather.9.cloned.1.call-start = ((), (), s32[]{:S(2)}) async-start(), calls=%async_computation.1 | async-start | bytes 2228224 | tf_op jit(solution)/shard_map/all_gather | solution.py:103
  576.7 556.6 %collective-permute-start.2 = (bf16[128,3072]{1,0:T(8,128)(2,1)}, bf16[128,3072]{1,0:T(8,128)(2,1)}, u32[]{:S(2)}, u32[]{:S(2)}) collective-permute-start(bf16[128,3072]{1,0:T(8,128)(2,1)} %param.7), channel_id=1, source_target_pairs={{0,1},{1,2},{2,3},{3,4},{4,5},{5,6},{6,7},{7,8},{8,9},{9,10},{10,1... | collective-permute-start | bytes 2359304 | tf_op jit(solution)/shard_map/ppermute | solution.py:20
  578.8 560.2 %collective-permute-start.1 = (bf16[128,3072]{0,1:T(8,128)(2,1)}, bf16[128,3072]{0,1:T(8,128)(2,1)}, u32[]{:S(2)}, u32[]{:S(2)}) collective-permute-start(bf16[128,3072]{0,1:T(8,128)(2,1)} %copy.80), channel_id=1, source_target_pairs={{0,1},{1,2},{2,3},{3,4},{4,5},{5,6},{6,7},{7,8},{8,9},{9,10},{10,1... | collective-permute-start | bytes 2359304 | tf_op jit(solution)/shard_map/ppermute | solution.py:20
  580.7 554.1 %collective-permute-start.5 = (bf16[128,3072]{1,0:T(8,128)(2,1)}, bf16[128,3072]{1,0:T(8,128)(2,1)}, u32[]{:S(2)}, u32[]{:S(2)}) collective-permute-start(bf16[128,3072]{1,0:T(8,128)(2,1)} %param.7), channel_id=1, source_target_pairs={{0,2},{1,3},{2,4},{3,5},{4,6},{5,7},{6,8},{7,9},{8,10},{9,11},{10,... | collective-permute-start | bytes 2359304 | tf_op jit(solution)/shard_map/ppermute | solution.py:20
  582.6 554.4 %collective-permute-start.4 = (bf16[128,3072]{0,1:T(8,128)(2,1)}, bf16[128,3072]{0,1:T(8,128)(2,1)}, u32[]{:S(2)}, u32[]{:S(2)}) collective-permute-start(bf16[128,3072]{0,1:T(8,128)(2,1)} %copy.80), channel_id=1, source_target_pairs={{0,2},{1,3},{2,4},{3,5},{4,6},{5,7},{6,8},{7,9},{8,10},{9,11},{10,... | collective-permute-start | bytes 2359304 | tf_op jit(solution)/shard_map/ppermute | solution.py:20
  584.6 530.5 %collective-permute-start = (bf16[128]{0:T(256)(128)(2,1)S(1)}, bf16[128]{0:T(256)(128)(2,1)S(1)}, u32[]{:S(2)}, u32[]{:S(2)}) collective-permute-start(bf16[128]{0:T(256)(128)(2,1)S(1)} %get-tuple-element.37), channel_id=1, source_target_pairs={{0,1},{1,2},{2,3},{3,4},{4,5},{5,6},{6,7},{7,8},{8,9},{9,10},{10,1... | collective-permute-start | bytes 776 | tf_op jit(solution)/shard_map/ppermute | solution.py:20
  1115.1 18.1 %collective-permute-start.3 = (bf16[128]{0:T(256)(128)(2,1)S(1)}, bf16[128]{0:T(256)(128)(2,1)S(1)}, u32[]{:S(2)}, u32[]{:S(2)}) collective-permute-start(bf16[128]{0:T(256)(128)(2,1)S(1)} %get-tuple-element.37), channel_id=1, source_target_pairs={{0,2},{1,3},{2,4},{3,5},{4,6},{5,7},{6,8},{7,9},{8,10},{9,11},{10,... | collective-permute-start | bytes 776 | tf_op jit(solution)/shard_map/ppermute | solution.py:20
  1141.0 1.1 copy-start.5
  1142.8 1.2 copy-start.1
  1150.6 2.0 copy-start.3
  1153.8 5.1 copy-start.4
  1156.8 2.1 copy-start
  1156.8 2.6 copy-start.2
  1156.8 3.6 copy-start.6
  1205.4 4.0 slice-start
Sparse Core Ops, SparseCore 0:
  15.2 561.3 all-reduce.2
Sparse Core Ops, SparseCore 1:
  17.7 107.5 all-gather.12
  127.1 84.2 all-gather.10
  576.7 299.0 all-gather.6
  1133.3 72.0 all-gather.8
where the time goes:
time: 1220 us
  waiting for transfers between devices  619 us (51%)
  blocking collectives  527 us (43%)
  local copies, waits for them, and re-layouts  21.1 us (2%)
  matrix products  16.4 us (1%)
  between operations  16.2 us (1%)
    psum x1, waiting for transfers between devices, spread(): return lax.psum(kept, axis)  559 us
    psum x1, blocking collectives, spread(): return lax.psum(kept, axis)  282 us
    all_gather x1, blocking collectives, on_device(): lax.all_gather(summary_here[2], 'grp', axis=0, tiled=True)  219 us
    all_gather x1, waiting for transfers between devices, on_device(): lax.all_gather(summary_here[1], 'grp', axis=0, tiled=True)  43.3 us
    all_gather x1, blocking collectives, on_device(): lax.all_gather(column_own[2], 'grp', axis=0, tiled=True)  25.1 us
  transfers between devices with their start and end apart: 11, of which 3 were waited for; matrix products, arithmetic and copies ran while one was open for 2% of the time, Pallas kernels for 0%

commit v1 on v0

--- a/solution.py
+++ b/solution.py
@@ -12,6 +12,13 @@
 BLOCK = 128
 LOOKBACK = 2
 NEG = -1e30
+
+
+def gather_over(x, name, d):
+    size = lax.axis_size(name)
+    shards = jnp.stack([x for _ in range(size)])
+    shards = lax.all_to_all(shards, name, split_axis=0, concat_axis=0)
+    return jnp.concatenate(shards, axis=d)
 
 
 def passed_along(block, axis, distance):
@@ -121,7 +128,7 @@
     shard_rows = (
         lax.all_gather(column_own[0], "grp", axis=0, tiled=True),
         lax.all_gather(column_own[1], "grp", axis=0, tiled=True),
-        lax.all_gather(column_own[2], "grp", axis=0, tiled=True),
+        gather_over(column_own[2], "grp", 0),
     )
     row_count = shard_rows[0].shape[0]
     row_window = jnp.arange(row_count, dtype=jnp.int32) // BLOCK

time: 1220 us -> 1190 us (0.975)
  blocking collectives: 527 us -> 472 us
  starting transfers between devices: 12.1 us -> 43.3 us
    all_gather x1, blocking collectives: 219 us -> 163 us  [on_device(): lax.all_gather(summary_here[2], 'grp', axis=0, tiled=True)]
    all_to_all x0 -> x1, starting transfers between devices: none -> 31.2 us  [gather_over(): shards = lax.all_to_all(shards, name, split_axis=0, concat_axis=0)]
    psum x1, blocking collectives: 282 us -> 309 us  [spread(): return lax.psum(kept, axis)]
    all_gather x1 -> x0, blocking collectives: 25.1 us -> none  [on_device(): lax.all_gather(column_own[2], 'grp', axis=0, tiled=True)]
  transfers between devices with their start and end apart: 11 -> 12, of which waited for: 3 -> 3; matrix products, arithmetic and copies ran while one was open for 2% -> 2% of each run, Pallas kernels for 0% -> 0%
where the time goes in v1:
time: 1190 us
  waiting for transfers between devices  618 us (52%)
  blocking collectives  472 us (40%)
  starting transfers between devices  43.3 us (4%)
  local copies, waits for them, and re-layouts  21.6 us (2%)
  matrix products  16.5 us (1%)
  between operations  16 us (1%)
    psum x1, waiting for transfers between devices, spread(): return lax.psum(kept, axis)  559 us
    psum x1, blocking collectives, spread(): return lax.psum(kept, axis)  309 us
    all_gather x1, blocking collectives, on_device(): lax.all_gather(summary_here[2], 'grp', axis=0, tiled=True)  163 us
    all_gather x1, waiting for transfers between devices, on_device(): lax.all_gather(summary_here[1], 'grp', axis=0, tiled=True)  42 us
    all_to_all x1, starting transfers between devices, gather_over(): shards = lax.all_to_all(shards, name, split_axis=0, concat_axis=0)  31.2 us
  transfers between devices with their start and end apart: 12, of which 3 were waited for; matrix products, arithmetic and copies ran while one was open for 2% of the time, Pallas kernels for 0%

profile of v1, /device:TPU:1, one launch (start us, length us, event | category | flops | bytes accessed | tf_op | source)
XLA Modules:
  0.0 1193.3 jit_solution(8748704284576065198)
XLA Ops:
  7.4 2.3 copy.108
  12.4 1.7 slice_select_fusion.1
  17.1 559.2 %all-reduce.3.cloned.1.call-done = (bf16[128,512]{0,1:T(8,128)(2,1)}, bf16[128,512]{0,1:T(8,128)(2,1)}) async-done(((bf16[128,512]{0,1:T(8,128)(2,1)}, bf16[128,512]{0,1:T(8,128)(2,1)}), (bf16[128,512]{0,1:T(8,128)(2,1)}, bf16[128,512]{0,1:T(8,128)(2,1)})) %all-reduce.3.cloned.1.call-update) | async-done | bytes 262160 | tf_op jit(solution)/shard_map/psum | solution.py:32
  576.3 2.1 collective-permute-start.2
  578.4 1.9 collective-permute-start.1
  580.3 1.9 collective-permute-start.5
  582.3 1.9 collective-permute-start.4
  584.2 1.9 collective-permute-start
  586.8 31.2 %all-to-all-start = ((bf16[16,1,128]{2,1,0:T(2,128)(2,1)}), bf16[16,1,128]{2,1,0:T(2,128)(2,1)S(1)}, u32[]{:S(2)}, u32[]{:S(2)}) async-start(bf16[16,1,128]{2,1,0:T(2,128)(2,1)} %stack.2), calls=%async_computation | async-start | bytes 16384 | tf_op jit(solution)/shard_map/all_to_all | solution.py:20
  618.5 308.5 %psum.21 = bf16[128]{0:T(256)(128)(2,1)S(1)} all-reduce(bf16[128]{0:T(256)(128)(2,1)S(1)} %broadcast_select_fusion), channel_id=1, replica_groups=mesh['grp'=16,'seq'=32] {'seq'}, use_global_device_ids=true, to_apply=%region_4.5 | all-reduce | flops 128 | bytes 512 | tf_op jit(solution)/shard_map/psum | solution.py:32
  927.0 163.0 %all-gather = bf16[16,1,128]{2,1,0:T(2,128)(2,1)S(1)} all-gather(bf16[1,1,128]{2,1,0:T(2,128)(2,1)S(1)} %bitcast.72), channel_id=1, replica_groups=mesh['grp'=16,'seq'=32] {'grp'}, dimensions={0}, use_global_device_ids=true | all-gather | bytes 4352 | tf_op jit(solution)/shard_map/all_gather | solution.py:111
  1091.3 2.1 collective-permute-start.3
  1093.5 16.0 %collective-permute-done.3 = bf16[128]{0:T(256)(128)(2,1)S(1)} collective-permute-done((bf16[128]{0:T(256)(128)(2,1)S(1)}, bf16[128]{0:T(256)(128)(2,1)S(1)}, u32[]{:S(2)}, u32[]{:S(2)}) %collective-permute-start.3) | collective-permute-done | bytes 288 | tf_op jit(solution)/shard_map/ppermute | solution.py:27
  1111.0 2.3 copy.116
  1113.3 1.6 fusion.96
  1115.2 1.6 fusion.94
  1120.2 3.9 copy.129
  1124.2 2.7 fusion.2
  1126.9 2.0 copy-done.3
  1130.1 2.9 bitcast_reduce_fusion
  1133.0 1.6 fusion.5
  1136.6 1.7 fusion.55
  1138.3 42.0 %all-gather.8.cloned.1.call-done = bf16[2048,512]{0,1:T(8,128)(2,1)} async-done(((bf16[128,512]{0,1:T(8,128)(2,1)}), bf16[2048,512]{0,1:T(8,128)(2,1)}) %all-gather.8.cloned.1.call-update) | async-done | bytes 2097168 | tf_op jit(solution)/shard_map/all_gather | solution.py:110
  1180.4 4.0 fusion.56
  (73 shorter events, 17.1 us)
Async XLA Ops:
  7.4 568.9 %all-reduce.3.cloned.1.call-start = ((), (), s32[]{:S(2)}) async-start(), calls=%async_computation.5 | async-start | bytes 524288 | tf_op jit(solution)/shard_map/psum | solution.py:32
  7.4 3.9 copy-start.9
  9.7 574.5 %copy-start.10 = (s32[128]{0:T(128)S(1)}, s32[128]{0:T(128)}, u32[]{:S(2)}) copy-start(s32[128]{0:T(128)} %param.8) | copy-start | bytes 1540
  9.7 608.4 %copy-start.7 = (bf16[128,3072]{1,0:T(8,128)(2,1)S(1)}, bf16[128,3072]{1,0:T(8,128)(2,1)}, u32[]{:S(2)}) copy-start(bf16[128,3072]{1,0:T(8,128)(2,1)} %param.5) | copy-start | bytes 2359300
  14.1 1076.1 %copy-start.8 = (bf16[128,3072]{1,0:T(8,128)(2,1)S(1)}, bf16[128,3072]{1,0:T(8,128)(2,1)}, u32[]{:S(2)}) copy-start(bf16[128,3072]{1,0:T(8,128)(2,1)} %param.6) | copy-start | bytes 2359300
  14.8 1105.4 %all-gather.12.cloned.1.call-start = ((), (), s32[]{:S(2)}) async-start(), calls=%async_computation.4 | async-start | bytes 2228224 | tf_op jit(solution)/shard_map/all_gather | solution.py:130
  16.4 1107.7 %all-gather.10.cloned.1.call-start = ((), (), s32[]{:S(2)}) async-start(), calls=%async_computation.3 | async-start | bytes 2228224 | tf_op jit(solution)/shard_map/all_gather | solution.py:129
  17.0 1113.0 %all-gather.6.cloned.1.call-start = ((), (), s32[]{:S(2)}) async-start(), calls=%async_computation.1 | async-start | bytes 2228224 | tf_op jit(solution)/shard_map/all_gather | solution.py:109
  576.3 533.2 %collective-permute-start.2 = (bf16[128,3072]{1,0:T(8,128)(2,1)}, bf16[128,3072]{1,0:T(8,128)(2,1)}, u32[]{:S(2)}, u32[]{:S(2)}) collective-permute-start(bf16[128,3072]{1,0:T(8,128)(2,1)} %param.7), channel_id=1, source_target_pairs={{0,1},{1,2},{2,3},{3,4},{4,5},{5,6},{6,7},{7,8},{8,9},{9,10},{10,1... | collective-permute-start | bytes 2359304 | tf_op jit(solution)/shard_map/ppermute | solution.py:27
  578.4 536.8 %collective-permute-start.1 = (bf16[128,3072]{0,1:T(8,128)(2,1)}, bf16[128,3072]{0,1:T(8,128)(2,1)}, u32[]{:S(2)}, u32[]{:S(2)}) collective-permute-start(bf16[128,3072]{0,1:T(8,128)(2,1)} %copy.108), channel_id=1, source_target_pairs={{0,1},{1,2},{2,3},{3,4},{4,5},{5,6},{6,7},{7,8},{8,9},{9,10},{10,1... | collective-permute-start | bytes 2359304 | tf_op jit(solution)/shard_map/ppermute | solution.py:27
  580.3 530.7 %collective-permute-start.5 = (bf16[128,3072]{1,0:T(8,128)(2,1)}, bf16[128,3072]{1,0:T(8,128)(2,1)}, u32[]{:S(2)}, u32[]{:S(2)}) collective-permute-start(bf16[128,3072]{1,0:T(8,128)(2,1)} %param.7), channel_id=1, source_target_pairs={{0,2},{1,3},{2,4},{3,5},{4,6},{5,7},{6,8},{7,9},{8,10},{9,11},{10,... | collective-permute-start | bytes 2359304 | tf_op jit(solution)/shard_map/ppermute | solution.py:27
  582.3 531.0 %collective-permute-start.4 = (bf16[128,3072]{0,1:T(8,128)(2,1)}, bf16[128,3072]{0,1:T(8,128)(2,1)}, u32[]{:S(2)}, u32[]{:S(2)}) collective-permute-start(bf16[128,3072]{0,1:T(8,128)(2,1)} %copy.108), channel_id=1, source_target_pairs={{0,2},{1,3},{2,4},{3,5},{4,6},{5,7},{6,8},{7,9},{8,10},{9,11},{10,... | collective-permute-start | bytes 2359304 | tf_op jit(solution)/shard_map/ppermute | solution.py:27
  584.2 507.1 %collective-permute-start = (bf16[128]{0:T(256)(128)(2,1)S(1)}, bf16[128]{0:T(256)(128)(2,1)S(1)}, u32[]{:S(2)}, u32[]{:S(2)}) collective-permute-start(bf16[128]{0:T(256)(128)(2,1)S(1)} %convert_element_type.33), channel_id=1, source_target_pairs={{0,1},{1,2},{2,3},{3,4},{4,5},{5,6},{6,7},{7,8},{8,9},{9,10},{10,1... | collective-permute-start | bytes 776 | tf_op jit(solution)/shard_map/ppermute | solution.py:27
  586.8 522.7 %all-to-all-start = ((bf16[16,1,128]{2,1,0:T(2,128)(2,1)}), bf16[16,1,128]{2,1,0:T(2,128)(2,1)S(1)}, u32[]{:S(2)}, u32[]{:S(2)}) async-start(bf16[16,1,128]{2,1,0:T(2,128)(2,1)} %stack.2), calls=%async_computation | async-start | bytes 16384 | tf_op jit(solution)/shard_map/all_to_all | solution.py:20
  618.0 562.4 %all-gather.8.cloned.1.call-start = ((), (), s32[]{:S(2)}) async-start(), calls=%async_computation.2 | async-start | bytes 2228224 | tf_op jit(solution)/shard_map/all_gather | solution.py:110
  1091.3 18.1 %collective-permute-start.3 = (bf16[128]{0:T(256)(128)(2,1)S(1)}, bf16[128]{0:T(256)(128)(2,1)S(1)}, u32[]{:S(2)}, u32[]{:S(2)}) collective-permute-start(bf16[128]{0:T(256)(128)(2,1)S(1)} %convert_element_type.33), channel_id=1, source_target_pairs={{0,2},{1,3},{2,4},{3,5},{4,6},{5,7},{6,8},{7,9},{8,10},{9,11},{10,... | collective-permute-start | bytes 776 | tf_op jit(solution)/shard_map/ppermute | solution.py:27
  1117.2 1.1 copy-start.5
  1119.0 1.2 copy-start.1
  1126.9 2.0 copy-start.3
  1130.0 5.1 copy-start.4
  1133.0 2.1 copy-start
  1133.0 2.6 copy-start.2
  1133.0 3.6 copy-start.6
  1180.4 4.0 slice-start
Sparse Core Ops, SparseCore 0:
  14.9 561.3 all-reduce.2
Sparse Core Ops, SparseCore 1:
  17.3 107.5 all-gather.11
  126.8 84.2 all-gather.9
  576.4 296.3 all-gather.5
  1109.6 70.7 all-gather.7
